TPU v7x, 512 devices: a whole 4x8x8 slice. The times are simulated.
512 devices in a mesh: seq: 32 (over z, x), rep: 16 (over y, core).
Axes of the slice: x: 4, y: 8, z: 8, core: 2. Of those that a mesh axis runs over, the one named last changes fastest.
Arguments:
- states: bfloat16 [98304, 512], P(('rep', 'seq')), parts along dimension 0, may hold values from -6 to 6
- starts: int32 [16384], P(('rep', 'seq')), parts along dimension 0, may hold values from 0 to 6143, as said below
- straddle: int32 [512], P(('rep', 'seq')), parts along dimension 0, may hold values from 0 to 63, as said below
- key_weight: bfloat16 [512, 512], replicated
- out_weight: bfloat16 [512, 4096], P(None, 'seq'), may hold values from -0.25 to 0.25
- norm_gain: bfloat16 [4096], P('seq'), may hold values from 0.25 to 1.75
- attn_weight: bfloat16 [4096, 3, 4096], P(None, None, 'seq')
Outputs:
- attended: bfloat16 [16384, 4096], P(('rep', 'seq')), parts along dimension 0
There are 16 independent parts, one for each index of `rep`. A program takes and returns all parts, laid end to end along the dimension named above; an argument that names none is the same for every part. Nothing has to cross between parts.
Inputs may be any that keep to these rules, and one draw needn't show every extreme that they name: Rising; shard s of 192 bytes holds the starts of exactly 32 patches, numbers s * 32 to (s+1) * 32 - 1; the first of them lies at most 63 bytes into the shard, and at byte 0 for shard 0. `straddle`: entry s equals the first start of shard s+1 minus (s+1) * 192; the last entry is 0.
All inputs are finite; a program needn't handle non-finite values.
Results may differ from a plain program's by a relative error of at most 0.0096.
Values may be sent and summed in bfloat16 or wider, within the bound.
No kernel may reach another device: no remote copies, remote signals or barrier semaphores. Data moves between devices by JAX's collectives and lax.ppermute only.
A program may use at most 64 MiB of HBM per device.

v0:
```python
import jax
import jax.numpy as jnp
from jax import lax
from jax.sharding import PartitionSpec as P

HD = 128
LHD = 128
HALO = 64
epsilon = 1e-05


def shifted(shard, axis, by):
    size = lax.axis_size(axis)
    pairs = [(i, i + by) for i in range(size) if 0 <= i + by < size]
    return lax.ppermute(shard, axis, pairs)


def cross_pool(window, local_starts, halo_count, key_weight, patch_total, head_size):
    window_rows = window.shape[0]
    shard_bytes = window_rows - HALO
    width = window.shape[1]
    head_count = width // head_size
    position = jnp.arange(window_rows, dtype=jnp.int32)
    patch_ends = jnp.concatenate([local_starts[1:], (shard_bytes + halo_count).reshape(1)])
    member = (position[None, :] >= local_starts[:, None]) & (
        position[None, :] < patch_ends[:, None]
    )
    byte_count = jnp.sum(member.astype(jnp.float32), axis=1)
    query = (
        jnp.dot(member.astype(jnp.bfloat16), window, preferred_element_type=jnp.float32)
        / byte_count[:, None]
    ).astype(jnp.bfloat16)
    keys = jnp.dot(window, key_weight, preferred_element_type=jnp.float32).astype(jnp.bfloat16)
    query_heads = query.reshape(patch_total, head_count, head_size)
    key_heads = keys.reshape(window_rows, head_count, head_size)
    scores = jnp.einsum(
        "phd,jhd->hpj", query_heads, key_heads, preferred_element_type=jnp.float32
    ) / jnp.sqrt(jnp.float32(head_size))
    scores = jnp.where(member[None], scores, jnp.float32(-1e30))
    row_peak = jnp.max(scores, axis=-1, keepdims=True)
    expo = jnp.where(member[None], jnp.exp(scores - row_peak), jnp.float32(0.0))
    cross = (expo / jnp.sum(expo, axis=-1, keepdims=True)).astype(jnp.bfloat16)
    value_heads = window.reshape(window_rows, head_count, head_size)
    pooled = jnp.einsum("hpj,jhd->phd", cross, value_heads, preferred_element_type=jnp.float32)
    return pooled.reshape(patch_total, width).astype(jnp.bfloat16)


def global_attend(head_view):
    patch_count = head_view.shape[0]
    scores = jnp.einsum(
        "qhd,khd->hqk", head_view[:, 0], head_view[:, 1], preferred_element_type=jnp.float32
    ) / jnp.sqrt(jnp.float32(HD))
    causal = jnp.arange(patch_count)[:, None] >= jnp.arange(patch_count)[None, :]
    scores = jnp.where(causal[None], scores, jnp.float32(-1e30))
    row_peak = jnp.max(scores, axis=-1, keepdims=True)
    expo = jnp.where(causal[None], jnp.exp(scores - row_peak), jnp.float32(0.0))
    probs = (expo / jnp.sum(expo, axis=-1, keepdims=True)).astype(jnp.bfloat16)
    attended = jnp.einsum(
        "hqk,khd->qhd", probs, head_view[:, 2], preferred_element_type=jnp.float32
    )
    return attended.reshape(patch_count, head_view.shape[2] * HD).astype(jnp.bfloat16)


def norm_rows(embedding, gain_row):
    meansq = jnp.mean(embedding * embedding, axis=1, keepdims=True)
    return (embedding * lax.rsqrt(meansq + epsilon) * gain_row.astype(jnp.float32)).astype(
        jnp.bfloat16
    )


def shards(states, starts, straddle, key_weight, out_weight, norm_gain, attn_weight):
    shard_index = lax.axis_index("seq")
    byte_rows = states.shape[0]
    patch_local = starts.shape[0]
    halo_rows = shifted(states[:HALO], "seq", -1)
    window = jnp.concatenate([states, halo_rows], axis=0)
    local_starts = starts - shard_index * byte_rows
    pooled = cross_pool(window, local_starts, straddle[0], key_weight, patch_local, LHD)
    local_width = attn_weight.shape[2]
    model_width = attn_weight.shape[0]
    proj_weight = attn_weight.reshape(model_width, 3 * local_width)
    out_full, gain_full = (
        lax.all_gather(out_weight, "seq", axis=1, tiled=True),
        lax.all_gather(norm_gain.reshape(1, -1), "seq", axis=1, tiled=True),
    )
    embedding = jnp.dot(pooled, out_full, preferred_element_type=jnp.float32)
    normed = norm_rows(embedding, gain_full)
    projected = jnp.dot(
        lax.all_gather(normed, "seq", axis=0, tiled=True),
        proj_weight,
        preferred_element_type=jnp.float32,
    ).astype(jnp.bfloat16)
    head_view = projected.reshape(projected.shape[0], 3, local_width // HD, HD)
    attended = global_attend(head_view)
    return lax.all_to_all(attended, "seq", split_axis=0, concat_axis=1, tiled=True)


def solution(mesh):
    placed = (
        P(("rep", "seq"), None),
        P(("rep", "seq")),
        P(("rep", "seq")),
        P(),
        P(None, "seq"),
        P("seq"),
        P(None, None, "seq"),
    )
    return jax.shard_map(
        shards, mesh=mesh, in_specs=placed, out_specs=P(("rep", "seq"), None), check_vma=False
    )
```

profile of v0, /device:TPU:8, one launch (start us, length us, event | category | flops | bytes accessed | tf_op | source)
XLA Modules:
  0.0 247.6 jit_solution(9140741254961553201)
XLA Ops:
  6.5 0.0 copy-start
  6.5 0.0 all-gather.5.cloned.1.call-start
  6.5 0.7 all-gather.5.cloned.1.call-update
  7.3 0.0 all-gather.7.cloned.1.call-start
  7.3 1.1 copy.29
  8.4 1.3 collective-permute-start
  10.3 0.7 broadcast_subtract_fusion
  11.0 0.1 slice.16
  11.1 46.9 %all-gather.1 = bf16[32,1,128]{2,1,0:T(2,128)(2,1)S(1)} all-gather(bf16[1,1,128]{2,1,0:T(2,128)(2,1)} %bitcast.62), channel_id=2, replica_groups=mesh['seq'=32,'rep'=16] {'seq'}, dimensions={0}, use_global_device_ids=true | all-gather | bytes 8448 | tf_op jit(solution)/shard_map/all_gather | solution.py:84
  58.0 0.1 pad_add_fusion
  58.1 0.1 fusion.23
  58.2 0.2 convert_reduce_fusion
  58.4 0.0 collective-permute-done
  58.4 0.1 pad_maximum_fusion
  58.5 0.2 fusion.13
  58.7 0.0 copy-done
  58.7 0.3 fusion.5
  59.0 0.4 fusion.28
  59.4 0.2 fusion.12
  59.6 44.0 %all-gather.5.cloned.1.call-done = bf16[512,4096]{1,0:T(8,128)(2,1)} async-done(((bf16[512,128]{1,0:T(8,128)(2,1)}), bf16[512,4096]{1,0:T(8,128)(2,1)}) %all-gather.5.cloned.1.call-update) | async-done | bytes 4194320 | tf_op jit(solution)/shard_map/all_gather | solution.py:83
  103.7 3.1 %multiply_reduce_fusion = (f32[32]{0:T(128)S(1)}, f32[32,4096]{1,0:T(8,128)S(1)}) fusion(bf16[512,4096]{1,0:T(8,128)(2,1)} %all-gather.5.cloned.1.call-done, bf16[4,4,8,128]{3,2,1,0:T(8,128)(2,1)S(1)} %fusion.12), kind=kOutput, calls=%fused_computation.24 | convolution fusion | flops 134479840 | bytes 4751488 | tf_op jit(solution)/shard_map/dot_general | solution.py:86
  106.8 0.8 multiply_convert_fusion
  107.7 0.0 all-gather.7.cloned.1.call-update
  107.7 4.7 %copy.34 = bf16[4096,3,128]{0,2,1:T(8,128)(2,1)} copy(bf16[4096,3,128]{2,0,1:T(8,128)(2,1)} %param.13) | data formatting | bytes 6291456 | tf_op args[6]
  112.4 100.1 %all-gather.7.cloned.1.call-done = bf16[1024,4096]{1,0:T(8,128)(2,1)} async-done(((bf16[32,4096]{1,0:T(8,128)(2,1)}), bf16[1024,4096]{1,0:T(8,128)(2,1)}) %all-gather.7.cloned.1.call-update) | async-done | bytes 8388624 | tf_op jit(solution)/shard_map/all_gather | solution.py:89
  212.5 7.7 %convolution_convert_fusion = bf16[1024,384]{0,1:T(8,128)(2,1)S(1)} fusion(bf16[1024,4096]{1,0:T(8,128)(2,1)} %all-gather.7.cloned.1.call-done, bf16[4096,384]{0,1:T(8,128)(2,1)} %bitcast.58), kind=kOutput, calls=%fused_computation.8 | convolution fusion | flops 3221618688 | bytes 12320768 | tf_op jit(solution)/shard_map/dot_general | solution.py:88
  220.2 0.8 fusion.1
  220.9 0.5 fusion.2
  221.4 0.8 fusion.6
  222.2 0.2 copy.35
  222.3 17.7 %all_to_all.16 = bf16[32,32,128]{2,1,0:T(8,128)(2,1)S(1)} all-to-all(bf16[32,32,128]{2,1,0:T(8,128)(2,1)S(1)} %bitcast.59), channel_id=1, replica_groups=mesh['seq'=32,'rep'=16] {'seq'}, dimensions={0} | all-to-all | bytes 524288 | tf_op jit(solution)/shard_map/all_to_all | solution.py:95
  240.0 0.7 copy_bitcast_fusion
  (3 shorter events, 0.0 us)
Async XLA Ops:
  6.5 52.2 %copy-start = (bf16[512,512]{1,0:T(8,128)(2,1)S(1)}, bf16[512,512]{1,0:T(8,128)(2,1)}, u32[]{:S(2)}) copy-start(bf16[512,512]{1,0:T(8,128)(2,1)} %param.10) | copy-start | bytes 1572868
  6.5 97.1 %all-gather.5.cloned.1.call-start = ((), (), s32[]{:S(2)}) async-start(), calls=%async_computation.1 | async-start | bytes 4325376 | tf_op jit(solution)/shard_map/all_gather | solution.py:83
  7.3 205.2 %all-gather.7.cloned.1.call-start = ((), (), s32[]{:S(2)}) async-start(), calls=%async_computation.2 | async-start | bytes 8650752 | tf_op jit(solution)/shard_map/all_gather | solution.py:89
  8.4 50.0 %collective-permute-start = (bf16[64,512]{0,1:T(8,128)(2,1)S(1)}, bf16[64,512]{0,1:T(8,128)(2,1)S(1)}, u32[]{:S(2)}, u32[]{:S(2)}) collective-permute-start(bf16[64,512]{0,1:T(8,128)(2,1)S(1)} %slice.20), channel_id=1, source_target_pairs={{16,0},{32,16},{48,32},{64,48},{80,64},{96,80},{112,96},{128,112},... | collective-permute-start | bytes 196616 | tf_op jit(solution)/shard_map/ppermute | solution.py:15
Sparse Core Ops, SparseCore 0:
  10.4 93.2 all-gather.4
  107.8 104.6 all-gather.6
where the time goes:
time: 248 us
  waiting for transfers between devices  145 us (58%)
  blocking collectives  64.6 us (26%)
  between operations  14.2 us (6%)
  matrix products  13.4 us (5%)
  local copies, waits for them, and re-layouts  6.75 us (3%)
    all_gather x1, waiting for transfers between devices, shards(): lax.all_gather(normed, 'seq', axis=0, tiled=True)  100 us
    all_gather x1, blocking collectives, shards(): lax.all_gather(norm_gain.reshape(1, -1), 'seq', axis=1, tiled=True)  46.9 us
    all_gather x1, waiting for transfers between devices, shards(): lax.all_gather(out_weight, 'seq', axis=1, tiled=True)  44 us
    all_to_all x1, blocking collectives, shards(): lax.all_to_all(attended, 'seq', split_axis=0, concat_axis=1, tiled=True)  17.7 us
    dot_general x1, matrix products, shards(): jnp.dot(lax.all_gather(normed, 'seq', axis=0, tiled=True), proj_weight, p...  7.71 us
    unnamed x4, local copies, waits for them, and re-layouts  5.78 us
  transfers between devices with their start and end apart: 3, of which 2 were waited for; matrix products, arithmetic and copies ran while one was open for 3% of the time, Pallas kernels for 0%

commit v1 on v0

--- a/solution.py
+++ b/solution.py
@@ -80,7 +80,9 @@
     model_width = attn_weight.shape[0]
     proj_weight = attn_weight.reshape(model_width, 3 * local_width)
     out_full, gain_full = (
-        lax.all_gather(out_weight, "seq", axis=1, tiled=True),
+        jnp.concatenate(
+            lax.all_to_all(jnp.stack([out_weight] * lax.axis_size("seq")), "seq", 0, 0), axis=1
+        ),
         lax.all_gather(norm_gain.reshape(1, -1), "seq", axis=1, tiled=True),
     )
     embedding = jnp.dot(pooled, out_full, preferred_element_type=jnp.float32)

time: 248 us -> 293 us (1.18)
  blocking collectives: 64.6 us -> 142 us
  waiting for transfers between devices: 145 us -> 97.1 us
  starting transfers between devices: 1.33 us -> 14.8 us
    all_gather x1, blocking collectives: 46.9 us -> 124 us  [shards(): lax.all_gather(norm_gain.reshape(1, -1), 'seq', axis=1, tiled=True)]
    all_gather x1 -> x0, waiting for transfers between devices: 44 us -> none  [shards(): lax.all_gather(out_weight, 'seq', axis=1, tiled=True)]
    all_to_all x0 -> x1, starting transfers between devices: none -> 13.4 us  [shards(): lax.all_to_all(jnp.stack([out_weight] * lax.axis_size('seq')), 'seq', 0, 0)]
    all_gather x1, waiting for transfers between devices: 100 us -> 97 us  [shards(): lax.all_gather(normed, 'seq', axis=0, tiled=True)]
    unnamed x4 -> x11, local copies, waits for them, and re-layouts: 5.78 us -> 5.93 us
  transfers between devices with their start and end apart: 3 -> 3, of which waited for: 2 -> 1; matrix products, arithmetic and copies ran while one was open for 3% -> 2% of each run, Pallas kernels for 0% -> 0%
where the time goes in v1:
time: 293 us
  blocking collectives  142 us (48%)
  waiting for transfers between devices  97.1 us (33%)
  starting transfers between devices  14.8 us (5%)
  between operations  14.2 us (5%)
  matrix products  13.9 us (5%)
  local copies, waits for them, and re-layouts  9.34 us (3%)
    all_gather x1, blocking collectives, shards(): lax.all_gather(norm_gain.reshape(1, -1), 'seq', axis=1, tiled=True)  124 us
    all_gather x1, waiting for transfers between devices, shards(): lax.all_gather(normed, 'seq', axis=0, tiled=True)  97 us
    all_to_all x1, blocking collectives, shards(): lax.all_to_all(attended, 'seq', split_axis=0, concat_axis=1, tiled=True)  17.7 us
    all_to_all x1, starting transfers between devices, shards(): lax.all_to_all(jnp.stack([out_weight] * lax.axis_size('seq')), 'seq', 0, 0)  13.4 us
    dot_general x1, matrix products, shards(): jnp.dot(lax.all_gather(normed, 'seq', axis=0, tiled=True), proj_weight, p...  7.71 us
    unnamed x11, local copies, waits for them, and re-layouts  5.93 us
  transfers between devices with their start and end apart: 3, of which 1 were waited for; matrix products, arithmetic and copies ran while one was open for 2% of the time, Pallas kernels for 0%

profile of v1, /device:TPU:8, one launch (start us, length us, event | category | flops | bytes accessed | tf_op | source)
XLA Modules:
  0.0 292.9 jit_solution(9941015017267827045)
XLA Ops:
  6.5 0.0 copy-start
  6.5 1.1 copy.36
  7.6 2.4 stack.2
  10.1 13.4 %all-to-all-start = ((bf16[32,512,128]{1,2,0:T(8,128)(2,1)}), bf16[32,512,128]{1,2,0:T(8,128)(2,1)}, u32[]{:S(2)}, u32[]{:S(2)}) async-start(bf16[32,512,128]{1,2,0:T(8,128)(2,1)} %stack.2), calls=%async_computation | async-start | bytes 8388608 | tf_op jit(solution)/shard_map/all_to_all | solution.py:84
  23.5 0.0 all-gather.4.cloned.1.call-start
  23.6 0.1 copy.31
  23.7 1.3 collective-permute-start
  25.7 0.0 copy-done.3
  25.7 0.1 slice.16
  25.8 124.1 %all-gather.1 = bf16[32,1,128]{2,1,0:T(2,128)(2,1)S(1)} all-gather(bf16[1,1,128]{2,1,0:T(2,128)(2,1)S(1)} %bitcast.65), channel_id=2, replica_groups=mesh['seq'=32,'rep'=16] {'seq'}, dimensions={0}, use_global_device_ids=true | all-gather | bytes 8448 | tf_op jit(solution)/shard_map/all_gather | solution.py:86
  149.8 0.1 pad_add_fusion
  149.9 0.1 fusion.23
  150.0 0.2 convert_reduce_fusion
  150.2 0.0 collective-permute-done
  150.2 0.1 pad_maximum_fusion
  150.3 0.2 fusion.13
  150.5 0.3 fusion.5
  150.9 0.4 fusion.28
  151.2 0.2 fusion.12
  151.4 0.0 all-to-all-done
  151.5 3.6 %multiply_reduce_fusion = (f32[32]{0:T(128)S(1)}, f32[32,4096]{1,0:T(8,128)S(1)}) fusion(bf16[512,4096]{0,1:T(8,128)(2,1)} %bitcast.3, bf16[4,4,8,128]{3,2,1,0:T(8,128)(2,1)S(1)} %fusion.12), kind=kOutput, calls=%fused_computation.24 | convolution fusion | flops 134479840 | bytes 4751488 | tf_op jit(solution)/shard_map/dot_general | solution.py:88
  155.1 0.8 multiply_convert_fusion
  155.9 0.0 all-gather.4.cloned.1.call-update
  156.0 4.7 %copy.37 = bf16[4096,3,128]{0,2,1:T(8,128)(2,1)} copy(bf16[4096,3,128]{2,0,1:T(8,128)(2,1)} %param.13) | data formatting | bytes 6291456 | tf_op args[6]
  160.7 97.0 %all-gather.4.cloned.1.call-done = bf16[1024,4096]{1,0:T(8,128)(2,1)} async-done(((bf16[32,4096]{1,0:T(8,128)(2,1)}), bf16[1024,4096]{1,0:T(8,128)(2,1)}) %all-gather.4.cloned.1.call-update) | async-done | bytes 8388624 | tf_op jit(solution)/shard_map/all_gather | solution.py:91
  257.7 7.7 %convolution_convert_fusion = bf16[1024,384]{0,1:T(8,128)(2,1)S(1)} fusion(bf16[1024,4096]{1,0:T(8,128)(2,1)} %all-gather.4.cloned.1.call-done, bf16[4096,384]{0,1:T(8,128)(2,1)} %bitcast.61), kind=kOutput, calls=%fused_computation.8 | convolution fusion | flops 3221618688 | bytes 12320768 | tf_op jit(solution)/shard_map/dot_general | solution.py:90
  265.4 0.8 fusion.1
  266.2 0.5 fusion.2
  266.7 0.8 fusion.6
  267.4 0.2 copy.38
  267.6 17.7 %all_to_all.21 = bf16[32,32,128]{2,1,0:T(8,128)(2,1)S(1)} all-to-all(bf16[32,32,128]{2,1,0:T(8,128)(2,1)S(1)} %bitcast.62), channel_id=1, replica_groups=mesh['seq'=32,'rep'=16] {'seq'}, dimensions={0} | all-to-all | bytes 524288 | tf_op jit(solution)/shard_map/all_to_all | solution.py:97
  285.3 0.7 copy_bitcast_fusion
  (10 shorter events, 0.0 us)
Async XLA Ops:
  6.5 144.0 %copy-start = (bf16[512,512]{1,0:T(8,128)(2,1)S(1)}, bf16[512,512]{1,0:T(8,128)(2,1)}, u32[]{:S(2)}) copy-start(bf16[512,512]{1,0:T(8,128)(2,1)} %param.10) | copy-start | bytes 1572868
  10.1 13.5 %copy-start.1 = (bf16[192,512]{1,0:T(8,128)(2,1)S(1)}, bf16[192,512]{1,0:T(8,128)(2,1)}, u32[]{:S(2)}) copy-start(bf16[192,512]{1,0:T(8,128)(2,1)} %param.7) | copy-start | bytes 589828
  10.1 15.6 %copy-start.3 = (s32[32]{0:T(128)S(1)}, s32[32]{0:T(128)}, u32[]{:S(2)}) copy-start(s32[32]{0:T(128)} %param.8) | copy-start | bytes 388
  10.1 15.7 %copy-start.2 = (bf16[128]{0:T(256)(128)(2,1)S(1)}, bf16[128]{0:T(256)(128)(2,1)}, u32[]{:S(2)}) copy-start(bf16[128]{0:T(256)(128)(2,1)} %param.12) | copy-start | bytes 772
  10.1 141.4 %all-to-all-start = ((bf16[32,512,128]{1,2,0:T(8,128)(2,1)}), bf16[32,512,128]{1,2,0:T(8,128)(2,1)}, u32[]{:S(2)}, u32[]{:S(2)}) async-start(bf16[32,512,128]{1,2,0:T(8,128)(2,1)} %stack.2), calls=%async_computation | async-start | bytes 8388608 | tf_op jit(solution)/shard_map/all_to_all | solution.py:84
  23.5 234.2 %all-gather.4.cloned.1.call-start = ((), (), s32[]{:S(2)}) async-start(), calls=%async_computation.2 | async-start | bytes 8650752 | tf_op jit(solution)/shard_map/all_gather | solution.py:91
  23.7 126.5 %collective-permute-start = (bf16[64,512]{0,1:T(8,128)(2,1)S(1)}, bf16[64,512]{0,1:T(8,128)(2,1)S(1)}, u32[]{:S(2)}, u32[]{:S(2)}) collective-permute-start(bf16[64,512]{0,1:T(8,128)(2,1)S(1)} %slice.20), channel_id=1, source_target_pairs={{16,0},{32,16},{48,32},{64,48},{80,64},{96,80},{112,96},{128,112},... | collective-permute-start | bytes 196616 | tf_op jit(solution)/shard_map/ppermute | solution.py:15
Sparse Core Ops, SparseCore 0:
  156.1 101.5 all-gather.3
